TPU v7x, 1024 devices: a whole 4x4x32 slice. The times are simulated.
1024 devices in a mesh: row: 8 (over x, core), col: 128 (over y, z).
Axes of the slice: x: 4, y: 4, z: 32, core: 2. Of those that a mesh axis runs over, the one named last changes fastest.
Arguments:
- inputs: bfloat16 [512, 8192], P('col', 'row'), may hold values from -1.5 to 1.5
- grad_out: bfloat16 [512, 8192], P('col', 'row'), may hold values from -3 to 3
- gate: bfloat16 [512, 30720], P('row', 'col'), may hold values from -6 to 6
- up: bfloat16 [512, 30720], P('row', 'col'), may hold values from -6 to 6
- gate_weight: bfloat16 [8192, 30720], P('row', 'col'), may hold values from -0.0625 to 0.0625
- up_weight: bfloat16 [8192, 30720], P('row', 'col'), may hold values from -0.0625 to 0.0625
- down_weight: bfloat16 [30720, 8192], P('col', 'row'), may hold values from -0.03125 to 0.03125
Outputs:
- grad_inputs: bfloat16 [512, 8192], P('col', 'row')
- grad_gate_weight: bfloat16 [8192, 30720], P('row', 'col')
- grad_up_weight: bfloat16 [8192, 30720], P('row', 'col')
- grad_down_weight: bfloat16 [30720, 8192], P('col', 'row')
All inputs are finite; a program needn't handle non-finite values.
Results may differ from a plain program's by a relative error of at most 0.022.
Values may be sent and summed in bfloat16 or wider, within the bound.
A program may use at most 32 MiB of HBM per device.

v0:
```python
import jax
import jax.numpy as jnp
from jax import lax
from jax.sharding import PartitionSpec as P


def swiglu_backward(grad_hidden, gate_part, up_part):
    gate_vals = gate_part.astype(jnp.float32)
    up_vals = up_part.astype(jnp.float32)
    sigmoid_gate = jax.nn.sigmoid(gate_vals)
    activated = gate_vals * sigmoid_gate
    grad_gate = (
        grad_hidden * up_vals * sigmoid_gate * (1.0 + gate_vals * (1.0 - sigmoid_gate))
    ).astype(jnp.bfloat16)
    grad_up = (grad_hidden * activated).astype(jnp.bfloat16)
    hidden = (activated * up_vals).astype(jnp.bfloat16)
    return (grad_gate, grad_up, hidden)


def local(inputs, grad_out, gate, up, gate_weight, up_weight, down_weight):
    out_all = lax.all_gather(grad_out, "col", axis=0, tiled=True)
    contract_last = (((1,), (1,)), ((), ()))
    contract_first = (((0,), (0,)), ((), ()))
    grad_hidden = lax.psum_scatter(
        lax.dot_general(
            out_all, down_weight, contract_last, preferred_element_type=jnp.float32
        ).astype(jnp.bfloat16),
        "row",
        scatter_dimension=0,
        tiled=True,
    ).astype(jnp.float32)
    grad_gate_own, grad_up_own, hidden_own = swiglu_backward(grad_hidden, gate, up)
    grad_gate_all, grad_up_all, hidden_all = (
        lax.all_gather(grad_gate_own, "row", axis=0, tiled=True),
        lax.all_gather(grad_up_own, "row", axis=0, tiled=True),
        lax.all_gather(hidden_own, "row", axis=0, tiled=True),
    )
    gate_rows = grad_gate_all
    up_rows = grad_up_all
    total = lax.dot_general(
        gate_rows, gate_weight, contract_last, preferred_element_type=jnp.float32
    )
    grad_inputs = lax.psum_scatter(
        total
        + lax.dot_general(up_rows, up_weight, contract_last, preferred_element_type=jnp.float32),
        "col",
        scatter_dimension=0,
        tiled=True,
    ).astype(jnp.bfloat16)
    grad_down = lax.dot_general(
        hidden_all, out_all, contract_first, preferred_element_type=jnp.float32
    )
    shard_rows = lax.all_gather(inputs, "col", axis=0, tiled=True)
    gate_rows = grad_gate_all
    up_rows = grad_up_all
    gate_total = lax.dot_general(
        shard_rows, gate_rows, contract_first, preferred_element_type=jnp.float32
    )
    up_total = lax.dot_general(
        shard_rows, up_rows, contract_first, preferred_element_type=jnp.float32
    )
    return (
        grad_inputs,
        gate_total.astype(jnp.bfloat16),
        up_total.astype(jnp.bfloat16),
        grad_down.astype(jnp.bfloat16),
    )


def solution(mesh):
    return jax.shard_map(
        local,
        mesh=mesh,
        in_specs=(
            P("col", "row"),
            P("col", "row"),
            P("row", "col"),
            P("row", "col"),
            P("row", "col"),
            P("row", "col"),
            P("col", "row"),
        ),
        out_specs=(P("col", "row"), P("row", "col"), P("row", "col"), P("col", "row")),
        check_vma=False,
    )
```

profile of v0, /device:TPU:4, one launch (start us, length us, event | category | flops | bytes accessed | tf_op | source)
XLA Modules:
  0.0 1185.6 jit_solution(7736745695901313302)
XLA Ops:
  7.2 0.0 copy-start
  7.2 0.0 copy-start.4
  7.2 0.0 all-gather.5.cloned.1.call-start
  7.2 0.7 all-gather.5.cloned.1.call-update
  7.9 0.0 all-gather.7.cloned.1.call-start
  8.0 0.7 all-gather.7.cloned.1.call-update
  8.7 0.0 reduce-scatter.2.cloned.1.call-start
  8.7 264.1 %all-gather.5.cloned.1.call-done = bf16[128,4,1024]{2,1,0:T(4,128)(2,1)} async-done(((bf16[1,4,1024]{2,1,0:T(4,128)(2,1)}), bf16[128,4,1024]{2,1,0:T(4,128)(2,1)}) %all-gather.5.cloned.1.call-update) | async-done | bytes 1048592 | tf_op jit(solution)/shard_map/all_gather | solution.py:21
  272.8 1.3 reshape.9
  274.1 0.0 copy-done.4
  274.1 0.0 copy-start.2
  274.1 0.0 copy-start.3
  274.2 1.2 convolution_convert_fusion.3
  275.3 0.0 reduce-scatter.2.cloned.1.call-update
  275.4 1.3 dynamic-slice
  277.3 242.9 %all-gather.7.cloned.1.call-done = bf16[128,4,1024]{2,1,0:T(4,128)(2,1)} async-done(((bf16[1,4,1024]{2,1,0:T(4,128)(2,1)}), bf16[128,4,1024]{2,1,0:T(4,128)(2,1)}) %all-gather.7.cloned.1.call-update) | async-done | bytes 1048592 | tf_op jit(solution)/shard_map/all_gather | solution.py:53
  520.2 1.3 reshape.11
  521.6 36.2 %reduce-scatter.2.cloned.1.call-done = bf16[64,240]{1,0:T(8,128)(2,1)} async-done(((bf16[512,240]{1,0:T(8,128)(2,1)}), bf16[64,240]{1,0:T(8,128)(2,1)}) %reduce-scatter.2.cloned.1.call-update) | async-done | bytes 30736 | tf_op jit(solution)/shard_map/reduce_scatter | solution.py:24
  557.7 0.0 copy-done.2
  557.7 0.0 copy-done.3
  557.7 0.8 fusion.6
  558.5 16.4 %all_gather.19 = bf16[512,240]{1,0:T(8,128)(2,1)S(1)} all-gather(bf16[64,240]{1,0:T(8,128)(2,1)S(1)} %get-tuple-element.4), channel_id=1, replica_groups=mesh['row'=8,'col'=128] {'row'}, dimensions={0}, use_global_device_ids=true | all-gather | bytes 276480 | tf_op jit(solution)/shard_map/all_gather | solution.py:36
  574.9 1.2 convolution_convert_fusion
  576.1 12.8 %all_gather.16 = bf16[512,240]{1,0:T(8,128)(2,1)S(1)} all-gather(bf16[64,240]{1,0:T(8,128)(2,1)S(1)} %get-tuple-element.5), channel_id=1, replica_groups=mesh['row'=8,'col'=128] {'row'}, dimensions={0}, use_global_device_ids=true | all-gather | bytes 276480 | tf_op jit(solution)/shard_map/all_gather | solution.py:34
  589.0 12.8 %all_gather.17 = bf16[512,240]{1,0:T(8,128)(2,1)S(1)} all-gather(bf16[64,240]{1,0:T(8,128)(2,1)S(1)} %get-tuple-element.6), channel_id=1, replica_groups=mesh['row'=8,'col'=128] {'row'}, dimensions={0}, use_global_device_ids=true | all-gather | bytes 276480 | tf_op jit(solution)/shard_map/all_gather | solution.py:35
  601.8 1.2 fusion.1
  603.0 0.0 copy-start.1
  603.0 1.2 fusion
  604.2 0.0 copy-done
  604.2 0.4 fusion.11
  604.7 0.0 copy-done.1
  604.7 0.4 convolution_add_fusion
  605.1 572.6 %all-reduce.2 = bf16[512,1024]{1,0:T(8,128)(2,1)} all-reduce(f32[512,1024]{1,0:T(8,128)S(1)} %convolution_add_fusion), channel_id=3, replica_groups=mesh['row'=8,'col'=128] {'col'}, use_global_device_ids=true, to_apply=%region_1.0.clone | all-reduce | flops 524288 | bytes 3145728
  1177.7 1.3 dynamic-slice_convert_fusion
Async XLA Ops:
  7.2 597.1 %copy-start = (bf16[1024,240]{0,1:T(8,128)(2,1)S(1)}, bf16[1024,240]{0,1:T(8,128)(2,1)}, u32[]{:S(2)}) copy-start(bf16[1024,240]{0,1:T(8,128)(2,1)} %param.11) | copy-start | bytes 1474564
  7.2 266.9 %copy-start.4 = (bf16[240,1024]{1,0:T(8,128)(2,1)S(1)}, bf16[240,1024]{1,0:T(8,128)(2,1)}, u32[]{:S(2)}) copy-start(bf16[240,1024]{1,0:T(8,128)(2,1)} %param.13) | copy-start | bytes 1474564
  7.2 265.6 %all-gather.5.cloned.1.call-start = ((), (), s32[]{:S(2)}) async-start(), calls=%async_computation.2 | async-start | bytes 1056768 | tf_op jit(solution)/shard_map/all_gather | solution.py:21
  7.9 512.3 %all-gather.7.cloned.1.call-start = ((), (), s32[]{:S(2)}) async-start(), calls=%async_computation.3 | async-start | bytes 1056768 | tf_op jit(solution)/shard_map/all_gather | solution.py:53
  8.7 549.0 %reduce-scatter.2.cloned.1.call-start = ((), (), s32[]{:S(2)}) async-start(), calls=%async_computation.1 | async-start | bytes 294912 | tf_op jit(solution)/shard_map/reduce_scatter | solution.py:24
  274.1 283.6 %copy-start.2 = (bf16[64,240]{1,0:T(8,128)(2,1)S(1)}, bf16[64,240]{1,0:T(8,128)(2,1)}, u32[]{:S(2)}) copy-start(bf16[64,240]{1,0:T(8,128)(2,1)} %param.10) | copy-start | bytes 92164
  274.1 283.6 %copy-start.3 = (bf16[64,240]{1,0:T(8,128)(2,1)S(1)}, bf16[64,240]{1,0:T(8,128)(2,1)}, u32[]{:S(2)}) copy-start(bf16[64,240]{1,0:T(8,128)(2,1)} %param.9) | copy-start | bytes 92164
  603.0 1.7 copy-start.1
Sparse Core Ops, SparseCore 0:
  12.1 260.6 all-gather.4
  276.8 243.3 all-gather.6
  524.2 33.5 reduce-scatter.1
where the time goes:
time: 1190 us
  blocking collectives  615 us (52%)
  waiting for transfers between devices  545 us (46%)
  between operations  14.5 us (1%)
    unnamed x1, blocking collectives  573 us
    all_gather x1, waiting for transfers between devices, local(): out_all = lax.all_gather(grad_out, 'col', axis=0, tiled=True)  264 us
    all_gather x1, waiting for transfers between devices, local(): shard_rows = lax.all_gather(inputs, 'col', axis=0, tiled=True)  243 us
    reduce_scatter x1, waiting for transfers between devices, local(): lax.psum_scatter(lax.dot_general(out_all, down_weight, contract_last, pre...  36.2 us
  transfers between devices with their start and end apart: 3, of which 3 were waited for; matrix products, arithmetic and copies ran while one was open for 0% of the time, Pallas kernels for 0%

commit v1 on v0

v1 whole, which is shorter than its diff:
```python
import jax
import jax.numpy as jnp
from jax import lax
from jax.experimental import pallas as pl
from jax.experimental.pallas import tpu as pltpu
from jax.sharding import PartitionSpec as P

MESH = pl.DeviceIdType.MESH
BF = jnp.bfloat16
F32 = jnp.float32

ROWS = 8
NY, NZ = 4, 32
NEAR, FAR = 4, 8
TOK = 4
TOKENS = 512
D = 1024
F = 240
H = D // 2
YB = 128
PB = 32
RB = 64


NT = (((1,), (1,)), ((), ()))
TN = (((0,), (0,)), ((), ()))


def al(x, n):
    return pl.multiple_of(x, n)


def kernel(
    in_hbm, out_hbm, gate_hbm, up_hbm, wg_hbm, wu_hbm, wd_hbm,
    gi_hbm, dwg_hbm, dwu_hbm, dwd_hbm,
    far_o, far_i, OUT, IN, wg, wu, wd, gate, up, fa, fb, hid,
    hp, hr, gh, gg, gu, s2, sp, sm, r2a, r2b, rm, rp, tb, sn, n1, n2, n3, n4,
    fs, fr, gi, dwg, dwu, dwd,
    ld_sem, st_sem,
    far_s, far_r, near_s, near_r, y_s, y_r, f_s, f_r,
    gu_s, gu_r, hp_s, hp_r, gh_s, gh_r,
    ry_s, ry_r, rn_s, rn_r, rf_s, rf_r,
):
    r = lax.axis_index("row")
    c = lax.axis_index("col")
    y = c // NZ
    z = c % NZ
    zl = z % NEAR
    zh = z // NEAR

    def at_z(dz):
        return (r, y * NZ + (z + dz + NZ) % NZ)

    def at_y(dy):
        return (r, ((y + dy + NY) % NY) * NZ + z)

    def at_row(dr):
        return ((r + dr) % ROWS, c)

    def remote(src, dst, ss, rs, dev):
        return pltpu.make_async_remote_copy(
            src_ref=src, dst_ref=dst, send_sem=ss, recv_sem=rs, device_id=dev, device_id_type=MESH
        )

    loads = [
        pltpu.make_async_copy(out_hbm, far_o.at[zh], ld_sem.at[0]),
        pltpu.make_async_copy(gate_hbm, gate.at[pl.ds(al(r * RB, RB), RB), :], ld_sem.at[1]),
        pltpu.make_async_copy(up_hbm, up.at[pl.ds(al(r * RB, RB), RB), :], ld_sem.at[2]),
        pltpu.make_async_copy(in_hbm, far_i.at[zh], ld_sem.at[3]),
        pltpu.make_async_copy(wd_hbm, wd, ld_sem.at[4]),
        pltpu.make_async_copy(wg_hbm, wg, ld_sem.at[5]),
        pltpu.make_async_copy(wu_hbm, wu, ld_sem.at[6]),
    ]
    for cp in loads:
        cp.start()

    barrier = pltpu.get_barrier_semaphore()
    partners = [at_z(NEAR * k) for k in range(1, FAR)] + [at_z(d) for d in (1, -1, 2, -2)]
    partners += [at_y(1), at_y(-1)] + [at_row(k) for k in range(1, ROWS)]
    for dev in partners:
        pl.semaphore_signal(barrier, inc=1, device_id=dev, device_id_type=MESH)
    pl.semaphore_wait(barrier, len(partners))

    pending = []

    def go(cp):
        cp.start()
        pending.append(cp)
        return cp

    def far_send(a, buf):
        return [
            go(remote(buf.at[zh], buf.at[zh], far_s.at[a, k], far_r.at[a, k], at_z(NEAR * k)))
            for k in range(1, FAR)
        ]

    def piece(yy, q):
        off = ((y + yy + NY) % NY) * YB + ((zl + q + NEAR) % NEAR) * PB
        return pl.ds(al(off, PB), PB)

    def far_done(a, cps, buf, full):
        for cp in cps:
            cp.wait_recv()
        for k in range(0, FAR, 4):
            block = jnp.concatenate([buf[k + j].astype(F32) for j in range(4)], axis=0)
            base = y * YB + zl * PB + k * TOK
            full[pl.ds(al(base, 4 * TOK), 4 * TOK), :] = block.astype(BF)

    LO, HI, ALL = pl.ds(0, H), pl.ds(H, H), pl.ds(0, D)

    def near_send(a, full):
        me = piece(0, 0)
        out = []
        for i, (dz, cols) in enumerate(((1, ALL), (-1, ALL), (2, LO), (-2, HI))):
            out.append(
                go(remote(full.at[me, cols], full.at[me, cols], near_s.at[a, i], near_r.at[a, i], at_z(dz)))
            )
        return out

    def y_send(a, full, q, i):
        rows = piece(0, q)
        return [
            go(remote(full.at[rows, :], full.at[rows, :], y_s.at[a, i, j], y_r.at[a, i, j], at_y(dy)))
            for j, dy in enumerate((1, -1))
        ]

    def y_forward(a, full, q, i, j):
        rows = piece(-1, q) if j == 0 else piece(1, q)
        cols = LO if j == 0 else HI
        return go(
            remote(full.at[rows, cols], full.at[rows, cols], f_s.at[a, i, j], f_r.at[a, i, j], at_y(1 if j == 0 else -1))
        )

    QS = (0, -1, 1, 2)

    loads[0].wait()
    far0 = far_send(0, far_o)

    loads[1].wait()
    loads[2].wait()
    mine = pl.ds(al(r * RB, RB), RB)
    gus = []
    for a, ref in enumerate((gate, up)):
        for k in range(1, ROWS):
            gus.append(go(remote(ref.at[mine, :], ref.at[mine, :], gu_s.at[a, k], gu_r.at[a, k], at_row(k))))

    far_done(0, far0, far_o, OUT)
    near0 = near_send(0, OUT)
    ys0 = [y_send(0, OUT, 0, 0)]
    near0[0].wait_recv()
    ys0.append(y_send(0, OUT, -1, 1))
    near0[1].wait_recv()
    ys0.append(y_send(0, OUT, 1, 2))
    near0[2].wait_recv()
    near0[3].wait_recv()
    ys0.append(y_send(0, OUT, 2, 3))

    loads[3].wait()
    far1 = far_send(1, far_i)

    for cp in gus:
        cp.wait_recv()
    ri = lax.broadcasted_iota(jnp.int32, (YB, YB), 0)
    ci = lax.broadcasted_iota(jnp.int32, (YB, YB), 1)
    want = ((ri // TOK) % FAR) * (NEAR * TOK) + (ri // PB) * TOK + ri % TOK
    perm = jnp.where(ci == want, 1.0, 0.0).astype(BF)
    for b in range(NY):
        rows = pl.ds(b * YB, YB)
        g = jnp.dot(perm, gate[rows, :], preferred_element_type=F32)
        u = jnp.dot(perm, up[rows, :], preferred_element_type=F32)
        s = 1.0 / (1.0 + jnp.exp(-g))
        act = g * s
        fa[rows, :] = u * s * (1.0 + g * (1.0 - s))
        fb[rows, :] = act
        hid[rows, :] = (act * u).astype(BF)

    loads[4].wait()
    hps = [None] * 8
    hp_of = {}

    def hidden_block(dy):
        yb = (y + dy + NY) % NY
        rows = pl.ds(al(yb * YB, YB), YB)
        part = lax.dot_general(OUT[rows, :], wd[...], NT, preferred_element_type=F32)
        hp[rows, :] = part.astype(BF)

    hidden_block(0)
    fw = []
    for i in range(4):
        ys0[i][0].wait_recv()
        fw.append(y_forward(0, OUT, QS[i], i, 0))
        ys0[i][1].wait_recv()
        fw.append(y_forward(0, OUT, QS[i], i, 1))
    hidden_block(-1)
    hidden_block(1)
    for cp in fw:
        cp.wait_recv()
    hidden_block(2)

    hpx = []
    for k in range(1, ROWS):
        dst_row = (r + k) % ROWS
        rows = pl.ds(al(dst_row * RB, RB), RB)
        hpx.append(go(remote(hp.at[rows, :], hr.at[k], hp_s.at[k], hp_r.at[k], at_row(k))))

    far_done(1, far1, far_i, IN)
    near1 = near_send(1, IN)
    ys1 = [y_send(1, IN, 0, 0)]

    acc = hp[mine, :].astype(F32)
    for k in range(1, ROWS):
        hpx[k - 1].wait_recv()
        acc = acc + hr[k].astype(F32)
    gh[mine, :] = acc.astype(BF)
    ghx = [go(remote(gh.at[mine, :], gh.at[mine, :], gh_s.at[k], gh_r.at[k], at_row(k))) for k in range(1, ROWS)]

    near1[0].wait_recv()
    ys1.append(y_send(1, IN, -1, 1))
    near1[1].wait_recv()
    ys1.append(y_send(1, IN, 1, 2))
    near1[2].wait_recv()
    near1[3].wait_recv()
    ys1.append(y_send(1, IN, 2, 3))

    for cp in ghx:
        cp.wait_recv()
    ghv = gh[...].astype(F32)
    gg[...] = (ghv * fa[...]).astype(BF)
    gu[...] = (ghv * fb[...]).astype(BF)
    loads[5].wait()
    loads[6].wait()

    def partial(dy):
        yb = (y + dy + NY) % NY
        rows = pl.ds(al(yb * YB, YB), YB)
        return lax.dot_general(gg[rows, :], wg[...], NT, preferred_element_type=F32) + lax.dot_general(
            gu[rows, :], wu[...], NT, preferred_element_type=F32
        )

    s2[...] = partial(2).astype(BF)
    ra = go(remote(s2.at[:, LO], r2a, ry_s.at[0], ry_r.at[0], at_y(1)))
    rb = go(remote(s2.at[:, HI], r2b, ry_s.at[1], ry_r.at[1], at_y(-1)))
    p1 = partial(1)
    m1 = partial(-1)
    tb[...] = partial(0)
    ra.wait_recv()
    sp[:, :H] = (p1[:, :H] + r2a[...].astype(F32)).astype(BF)
    sp[:, H:] = p1[:, H:].astype(BF)
    rpl = go(remote(sp, rm, ry_s.at[2], ry_r.at[2], at_y(1)))
    rb.wait_recv()
    sm[:, :H] = m1[:, :H].astype(BF)
    sm[:, H:] = (m1[:, H:] + r2b[...].astype(F32)).astype(BF)
    rmi = go(remote(sm, rp, ry_s.at[3], ry_r.at[3], at_y(-1)))

    dwd[...] = lax.dot_general(hid[...], OUT[...], TN, preferred_element_type=F32).astype(BF)
    st2 = pltpu.make_async_copy(dwd, dwd_hbm, st_sem.at[0])
    st2.start()

    rpl.wait_recv()
    rmi.wait_recv()
    tb[...] = tb[...] + rm[...].astype(F32) + rp[...].astype(F32)
    sn[...] = tb[...].astype(BF)

    def local_piece(q):
        return pl.ds(al(((zl + q + NEAR) % NEAR) * PB, PB), PB)

    nx = [
        go(remote(sn.at[local_piece(1), :], n1, rn_s.at[0], rn_r.at[0], at_z(1))),
        go(remote(sn.at[local_piece(-1), :], n2, rn_s.at[1], rn_r.at[1], at_z(-1))),
        go(remote(sn.at[local_piece(2), LO], n3, rn_s.at[2], rn_r.at[2], at_z(2))),
        go(remote(sn.at[local_piece(2), HI], n4, rn_s.at[3], rn_r.at[3], at_z(-2))),
    ]

    fw1 = []
    for i in range(4):
        ys1[i][0].wait_recv()
        fw1.append(y_forward(1, IN, QS[i], i, 0))
        ys1[i][1].wait_recv()
        fw1.append(y_forward(1, IN, QS[i], i, 1))

    for cp in nx:
        cp.wait_recv()
    own = tb[local_piece(0), :] + n1[...].astype(F32) + n2[...].astype(F32)
    lo = own[:, :H] + n3[...].astype(F32)
    hi = own[:, H:] + n4[...].astype(F32)
    for k in range(FAR):
        fs[k, :, :H] = lo[k * TOK:(k + 1) * TOK, :].astype(BF)
        fs[k, :, H:] = hi[k * TOK:(k + 1) * TOK, :].astype(BF)
    fx = []
    for k in range(1, FAR):
        dst = (zh + k) % FAR
        fx.append(go(remote(fs.at[dst], fr.at[k], rf_s.at[k], rf_r.at[k], at_z(NEAR * k))))

    for cp in fw1:
        cp.wait_recv()
    dwg[...] = lax.dot_general(IN[...], gg[...], TN, preferred_element_type=F32).astype(BF)
    st0 = pltpu.make_async_copy(dwg, dwg_hbm, st_sem.at[1])
    st0.start()
    dwu[...] = lax.dot_general(IN[...], gu[...], TN, preferred_element_type=F32).astype(BF)
    st1 = pltpu.make_async_copy(dwu, dwu_hbm, st_sem.at[2])
    st1.start()

    total = fs[zh].astype(F32)
    for k in range(1, FAR):
        fx[k - 1].wait_recv()
        total = total + fr[k].astype(F32)
    gi[...] = total.astype(BF)
    st3 = pltpu.make_async_copy(gi, gi_hbm, st_sem.at[3])
    st3.start()

    for cp in pending:
        cp.wait_send()
    for cp in (st0, st1, st2, st3):
        cp.wait()


def local(inputs, grad_out, gate, up, gate_weight, up_weight, down_weight):
    anyspec = pl.BlockSpec(memory_space=pl.ANY)
    V = pltpu.VMEM
    dma = pltpu.SemaphoreType.DMA
    scratch = [
        V((FAR, TOK, D), BF), V((FAR, TOK, D), BF),
        V((TOKENS, D), BF), V((TOKENS, D), BF),
        V((D, F), BF), V((D, F), BF), V((F, D), BF),
        V((TOKENS, F), BF), V((TOKENS, F), BF),
        V((TOKENS, F), F32), V((TOKENS, F), F32), V((TOKENS, F), BF),
        V((TOKENS, F), BF), V((ROWS, RB, F), BF), V((TOKENS, F), BF),
        V((TOKENS, F), BF), V((TOKENS, F), BF),
        V((YB, D), BF), V((YB, D), BF), V((YB, D), BF),
        V((YB, H), BF), V((YB, H), BF), V((YB, D), BF), V((YB, D), BF),
        V((YB, D), F32), V((YB, D), BF),
        V((PB, D), BF), V((PB, D), BF), V((PB, H), BF), V((PB, H), BF),
        V((FAR, TOK, D), BF), V((FAR, TOK, D), BF), V((TOK, D), BF),
        V((D, F), BF), V((D, F), BF), V((F, D), BF),
        dma((7,)), dma((4,)),
        dma((2, FAR)), dma((2, FAR)), dma((2, 4)), dma((2, 4)),
        dma((2, 4, 2)), dma((2, 4, 2)), dma((2, 4, 2)), dma((2, 4, 2)),
        dma((2, ROWS)), dma((2, ROWS)), dma((ROWS,)), dma((ROWS,)), dma((ROWS,)), dma((ROWS,)),
        dma((4,)), dma((4,)), dma((4,)), dma((4,)), dma((FAR,)), dma((FAR,)),
    ]
    return pl.pallas_call(
        kernel,
        out_shape=(
            jax.ShapeDtypeStruct((TOK, D), BF),
            jax.ShapeDtypeStruct((D, F), BF),
            jax.ShapeDtypeStruct((D, F), BF),
            jax.ShapeDtypeStruct((F, D), BF),
        ),
        in_specs=[anyspec] * 7,
        out_specs=[anyspec] * 4,
        scratch_shapes=scratch,
        compiler_params=pltpu.CompilerParams(
            collective_id=0, has_side_effects=True, vmem_limit_bytes=48 * 1024 * 1024
        ),
    )(inputs, grad_out, gate, up, gate_weight, up_weight, down_weight)


def solution(mesh):
    return jax.shard_map(
        local,
        mesh=mesh,
        in_specs=(
            P("col", "row"), P("col", "row"), P("row", "col"), P("row", "col"),
            P("row", "col"), P("row", "col"), P("col", "row"),
        ),
        out_specs=(P("col", "row"), P("row", "col"), P("row", "col"), P("col", "row")),
        check_vma=False,
    )
```

time: 1190 us -> 110 us (0.09)
  the two profiles are of different devices: /device:TPU:4 before, /device:TPU:24 now
where the time goes in v1:
time: 110 us; the launch traced here: 109 us
  Pallas kernels  102 us (93%)
  local copies, waits for them, and re-layouts  5.63 us (5%)
    pallas_call x1, Pallas kernels, local(): pl.pallas_call(kernel, out_shape=(jax.ShapeDtypeStruct((TOK, D), BF), jax...  102 us
    unnamed x16, local copies, waits for them, and re-layouts  3.67 us

profile of v1, /device:TPU:24, one launch (start us, length us, event | category | flops | bytes accessed | tf_op | source)
XLA Modules:
  0.0 108.7 jit_solution(14863306963201504505)
XLA Ops:
  0.6 0.0 copy-start.5
  0.6 1.3 %copy.11.wg_hbm = bf16[1024,240]{1,0:T(8,128)(2,1)S(1)} copy(bf16[1024,240]{0,1:T(8,128)(2,1)} %param.11) | data formatting | bytes 983040 | tf_op args[4]
  1.9 0.0 copy-done.5
  1.9 0.0 copy-start
  2.0 0.0 copy-start.1
  2.0 0.0 copy-start.2
  2.0 0.0 copy-start.3
  2.0 0.0 copy-start.4
  2.0 0.2 copy.12.wu_hbm
  2.2 0.8 copy-done
  3.0 0.0 copy-done.1
  3.0 0.0 copy-done.2
  3.0 0.0 copy-done.3
  3.0 0.0 copy-done.4
  3.0 102.4 %shard_map.102 = (bf16[4,1024]{1,0:T(4,128)(2,1)S(1)}, bf16[1024,240]{1,0:T(8,128)(2,1)S(1)}, bf16[1024,240]{1,0:T(8,128)(2,1)S(1)}, bf16[240,1024]{1,0:T(8,128)(2,1)S(1)}) custom-call(bf16[4,1024]{1,0:T(4,128)(2,1)S(1)} %copy-done.3, bf16[4,1024]{1,0:T(4,128)(2,1)S(1)} %copy-done.4, bf16[64,240]{1,0:T(8,128)(2,1)S(1)} %copy-done.1, ...), custom_call_target="tpu_custom_call" | custom-call | tf_op jit(solution)/shard_map/pallas_call | solution.py:341
  105.3 1.0 copy.13
  106.3 1.0 copy.14
  107.3 0.6 copy.17
  107.9 0.8 copy.18
Async XLA Ops:
  0.6 1.3 %copy-start.5 = (bf16[1024,240]{0,1:T(8,128)(2,1)S(1)}, bf16[1024,240]{0,1:T(8,128)(2,1)}, u32[]{:S(2)}) copy-start(bf16[1024,240]{0,1:T(8,128)(2,1)} %param.12) | copy-start | bytes 1474564
  1.9 1.0 copy-start
  2.0 1.0 copy-start.1
  2.0 1.0 copy-start.2
  2.0 1.0 copy-start.3
  2.0 1.0 copy-start.4

commit v2 on v1

v2 whole, which is shorter than its diff:
```python
import jax
import jax.numpy as jnp
from jax import lax
from jax.experimental import pallas as pl
from jax.experimental.pallas import tpu as pltpu
from jax.sharding import PartitionSpec as P

MESH = pl.DeviceIdType.MESH
BF = jnp.bfloat16
F32 = jnp.float32

ROWS = 8
NY, NZ = 4, 32
NEAR, FAR = 4, 8
TOK = 4
TOKENS = 512
D = 1024
F = 240
H = D // 2
YB = 128
PB = 32
RB = 64
EB = YB // 8


NT = (((1,), (1,)), ((), ()))
TN = (((0,), (0,)), ((), ()))


def al(x, n):
    return pl.multiple_of(x, n)


def kernel(
    in_hbm, out_hbm, gate_hbm, up_hbm, wg_hbm, wu_hbm, wd_hbm,
    gi, dwg, dwu, dwd,
    far_o, far_i, OUT, IN, wg, wu, wd, gate, up, fa, fb, hid,
    hp0, hpa, hpb, hr0, hra, hrb, gh0, gha, ghb, gg, gu, s2, sp, sm, r2, rm, rp, tb, sn, n1, n2, n3, n4,
    fs, ff, c1p, c1m, c2p, c2m, c3p, c3m, c4l, c4h, e2p, e2m,
    ld_sem,
    far_s, far_r, fw_s, fw_r, near_s, near_r, y_s, y_r, f_s, f_r,
    gu_s, gu_r, hp_s, hp_r, gh_s, gh_r,
    ry_s, ry_r, rn_s, rn_r, rf_s, rf_r,
):
    r = lax.axis_index("row")
    c = lax.axis_index("col")
    y = c // NZ
    z = c % NZ
    zl = z % NEAR
    zh = z // NEAR

    def at_z(dz):
        return (r, y * NZ + (z + dz + NZ) % NZ)

    def at_y(dy):
        return (r, ((y + dy + NY) % NY) * NZ + z)

    def at_row(dr):
        return ((r + dr) % ROWS, c)

    def remote(src, dst, ss, rs, dev):
        return pltpu.make_async_remote_copy(
            src_ref=src, dst_ref=dst, send_sem=ss, recv_sem=rs, device_id=dev, device_id_type=MESH
        )

    barrier = pltpu.get_barrier_semaphore()
    partners = [at_z(d) for d in (8, -8, 4, -4, 2, -2, 1, -1)] + [at_y(d) for d in (2, 1, -1)]
    partners += [at_row(k) for k in range(1, ROWS)]
    for dev in partners:
        pl.semaphore_signal(barrier, inc=1, device_id=dev, device_id_type=MESH)

    loads = [
        pltpu.make_async_copy(out_hbm, far_o.at[zh], ld_sem.at[0]),
        pltpu.make_async_copy(gate_hbm, gate.at[pl.ds(al(r * RB, RB), RB), :], ld_sem.at[1]),
        pltpu.make_async_copy(up_hbm, up.at[pl.ds(al(r * RB, RB), RB), :], ld_sem.at[2]),
        pltpu.make_async_copy(in_hbm, far_i.at[zh], ld_sem.at[3]),
        pltpu.make_async_copy(wd_hbm, wd, ld_sem.at[4]),
        pltpu.make_async_copy(wg_hbm, wg, ld_sem.at[5]),
        pltpu.make_async_copy(wu_hbm, wu, ld_sem.at[6]),
    ]
    for cp in loads:
        cp.start()
    loads[0].wait()
    pl.semaphore_wait(barrier, len(partners))

    pending = []

    def go(cp):
        cp.start()
        pending.append(cp)
        return cp

    LO, HI, ALL = pl.ds(0, H), pl.ds(H, H), pl.ds(0, D)

    def far_direct(a, buf):
        return [
            go(remote(buf.at[zh], buf.at[zh], far_s.at[a, j], far_r.at[a, j], at_z(NEAR * d)))
            for j, d in enumerate((2, -2, 1, -1))
        ]

    def far_forward(a, buf, direct):
        out = []
        for j, (d, cols) in enumerate(((1, LO), (-1, HI))):
            direct[j].wait_recv()
            slot = (zh - 2 * d + FAR) % FAR
            out.append(go(remote(buf.at[slot], buf.at[slot], fw_s.at[a, j, 0], fw_r.at[a, j, 0], at_z(NEAR * d))))
            out.append(
                go(
                    remote(
                        buf.at[slot, :, cols], buf.at[slot, :, cols],
                        fw_s.at[a, j, 1], fw_r.at[a, j, 1], at_z(2 * NEAR * d),
                    )
                )
            )
        return out

    def piece(yy, q):
        off = ((y + yy + NY) % NY) * YB + ((zl + q + NEAR) % NEAR) * PB
        return pl.ds(al(off, PB), PB)

    def far_done(cps, buf, full):
        for cp in cps:
            cp.wait_recv()
        for k in range(0, FAR, 4):
            block = jnp.concatenate([buf[k + j].astype(F32) for j in range(4)], axis=0)
            base = y * YB + zl * PB + k * TOK
            full[pl.ds(al(base, 4 * TOK), 4 * TOK), :] = block.astype(BF)

    def near_send(a, full):
        me = piece(0, 0)
        return [
            go(remote(full.at[me, cols], full.at[me, cols], near_s.at[a, i], near_r.at[a, i], at_z(dz)))
            for i, (dz, cols) in enumerate(((1, ALL), (-1, ALL), (2, LO), (-2, HI)))
        ]

    def y_send(a, full, q, i):
        rows = piece(0, q)
        return [
            go(remote(full.at[rows, :], full.at[rows, :], y_s.at[a, i, j], y_r.at[a, i, j], at_y(dy)))
            for j, dy in enumerate((1, -1))
        ]

    def y_forward(a, full, q, i, j):
        rows = piece(-1, q) if j == 0 else piece(1, q)
        cols = LO if j == 0 else HI
        return go(
            remote(full.at[rows, cols], full.at[rows, cols], f_s.at[a, i, j], f_r.at[a, i, j], at_y(1 if j == 0 else -1))
        )

    def near_to_y(a, full, near, ys):
        near[0].wait_recv()
        ys.append(y_send(a, full, -1, 1))
        near[1].wait_recv()
        ys.append(y_send(a, full, 1, 2))
        near[2].wait_recv()
        near[3].wait_recv()
        ys.append(y_send(a, full, 2, 3))

    def forwards(a, full, ys):
        fw = []
        for i in range(4):
            for j in range(2):
                ys[i][j].wait_recv()
                fw.append(y_forward(a, full, QS[i], i, j))
        return fw

    QS = (0, -1, 1, 2)

    far0 = far_direct(0, far_o)

    loads[1].wait()
    loads[2].wait()
    mine = pl.ds(al(r * RB, RB), RB)
    gus = []
    for a, ref in enumerate((gate, up)):
        for k in range(1, ROWS):
            gus.append(go(remote(ref.at[mine, :], ref.at[mine, :], gu_s.at[a, k], gu_r.at[a, k], at_row(k))))

    ffw0 = far_forward(0, far_o, far0)
    far_done(far0[2:] + ffw0, far_o, OUT)
    near0 = near_send(0, OUT)
    ys0 = [y_send(0, OUT, 0, 0)]
    near_to_y(0, OUT, near0, ys0)
    loads[3].wait()
    far1 = far_direct(1, far_i)

    for cp in gus:
        cp.wait_recv()
    ri = lax.broadcasted_iota(jnp.int32, (YB, YB), 0)
    ci = lax.broadcasted_iota(jnp.int32, (YB, YB), 1)
    want = ((ri // TOK) % FAR) * (NEAR * TOK) + (ri // PB) * TOK + ri % TOK
    perm = jnp.where(ci == want, 1.0, 0.0).astype(BF)
    for b in range(NY):
        rows = pl.ds(b * YB, YB)
        g = jnp.dot(perm, gate[rows, :], preferred_element_type=F32)
        u = jnp.dot(perm, up[rows, :], preferred_element_type=F32)
        s = 1.0 / (1.0 + jnp.exp(-g))
        act = g * s
        fa[rows, :] = u * s * (1.0 + g * (1.0 - s))
        fb[rows, :] = act
        hid[rows, :] = (act * u).astype(BF)

    loads[4].wait()

    def y_rows(dy):
        return pl.ds(al(((y + dy + NY) % NY) * YB, YB), YB)

    def hidden_block(dy, dst, i):
        part = lax.dot_general(OUT[y_rows(dy), :], wd[...], NT, preferred_element_type=F32)
        dst[:, i * EB:(i + 1) * EB, :] = part.astype(BF).reshape(ROWS, EB, F)

    def row_out(src, dst, b):
        cps = []
        for k in range(1, ROWS):
            cps.append(go(remote(src.at[(r + k) % ROWS], dst.at[k], hp_s.at[b, k], hp_r.at[b, k], at_row(k))))
        return cps

    def row_back(cps, own, got, dst, b):
        acc = own[r].astype(F32)
        for k in range(1, ROWS):
            cps[k - 1].wait_recv()
            acc = acc + got[k].astype(F32)
        dst[r] = acc.astype(BF)
        return [go(remote(dst.at[r], dst.at[r], gh_s.at[b, k], gh_r.at[b, k], at_row(k))) for k in range(1, ROWS)]

    def gated(dy, src, i):
        rows = y_rows(dy)
        v = src[:, i * EB:(i + 1) * EB, :].reshape(YB, F).astype(F32)
        gg[rows, :] = (v * fa[rows, :]).astype(BF)
        gu[rows, :] = (v * fb[rows, :]).astype(BF)

    def partial(dy):
        rows = y_rows(dy)
        return jnp.dot(gg[rows, :], wg[...], preferred_element_type=F32) + jnp.dot(
            gu[rows, :], wu[...], preferred_element_type=F32
        )

    hidden_block(0, hp0, 0)
    x0 = row_out(hp0, hr0, 0)
    fw0 = forwards(0, OUT, ys0)
    hidden_block(-1, hpa, 0)
    hidden_block(1, hpa, 1)
    xa = row_out(hpa, hra, 1)
    g0 = row_back(x0, hp0, hr0, gh0, 0)
    ffw1 = far_forward(1, far_i, far1)
    for cp in fw0:
        cp.wait_recv()
    hidden_block(2, hpb, 0)
    xb = row_out(hpb, hrb, 2)
    ga = row_back(xa, hpa, hra, gha, 1)
    gb = row_back(xb, hpb, hrb, ghb, 2)
    far_done(far1[2:] + ffw1, far_i, IN)
    near1 = near_send(1, IN)

    loads[5].wait()
    loads[6].wait()
    for cp in ga:
        cp.wait_recv()
    gated(1, gha, 1)
    sp[...] = partial(1).astype(BF)
    go_p = go(remote(sp, rm, ry_s.at[0], ry_r.at[0], at_y(1)))
    gated(-1, gha, 0)
    sm[...] = partial(-1).astype(BF)
    go_m = go(remote(sm, rp, ry_s.at[1], ry_r.at[1], at_y(-1)))
    for cp in g0:
        cp.wait_recv()
    gated(0, gh0, 0)
    tb[...] = partial(0)
    for cp in gb:
        cp.wait_recv()
    gated(2, ghb, 0)

    def local_piece(q):
        return pl.ds(al(((zl + q + NEAR) % NEAR) * PB, PB), PB)

    RQ = (2, 1, -1, 0)
    s2[...] = partial(2).astype(BF)
    far_y = [
        go(remote(s2.at[local_piece(q), :], r2.at[local_piece(q), :], ry_s.at[2 + i], ry_r.at[2 + i], at_y(2)))
        for i, q in enumerate(RQ)
    ]
    ys1 = [y_send(1, IN, 0, 0)]
    near_to_y(1, IN, near1, ys1)
    dwd[...] = lax.dot_general(hid[...], OUT[...], TN, preferred_element_type=F32).astype(BF)

    go_p.wait_recv()
    go_m.wait_recv()
    tb[...] = tb[...] + rm[...].astype(F32) + rp[...].astype(F32)
    nx = []
    for i, q in enumerate(RQ):
        rows = local_piece(q)
        far_y[i].wait_recv()
        v = tb[rows, :] + r2[rows, :].astype(F32)
        if q == 0:
            tb[rows, :] = v
            continue
        sn[rows, :] = v.astype(BF)
        if q == 2:
            nx.append(go(remote(sn.at[rows, LO], n3, rn_s.at[2], rn_r.at[2], at_z(2))))
            nx.append(go(remote(sn.at[rows, HI], n4, rn_s.at[3], rn_r.at[3], at_z(-2))))
        elif q == 1:
            nx.append(go(remote(sn.at[rows, :], n1, rn_s.at[0], rn_r.at[0], at_z(1))))
        else:
            nx.append(go(remote(sn.at[rows, :], n2, rn_s.at[1], rn_r.at[1], at_z(-1))))

    for cp in nx:
        cp.wait_recv()
    own = tb[local_piece(0), :] + n1[...].astype(F32) + n2[...].astype(F32)
    lo = own[:, :H] + n3[...].astype(F32)
    hi = own[:, H:] + n4[...].astype(F32)
    for k in range(FAR):
        ff[k, :, :H] = lo[k * TOK:(k + 1) * TOK, :]
        ff[k, :, H:] = hi[k * TOK:(k + 1) * TOK, :]
    for k in range(FAR):
        fs[k] = ff[k].astype(BF)

    def dest(d):
        return (zh + d + FAR) % FAR

    x4l = go(remote(fs.at[dest(4), :, LO], c4l, rf_s.at[0], rf_r.at[0], at_z(2 * NEAR)))
    x4h = go(remote(fs.at[dest(4), :, HI], c4h, rf_s.at[1], rf_r.at[1], at_z(-2 * NEAR)))
    x3p = go(remote(fs.at[dest(3)], c3p, rf_s.at[2], rf_r.at[2], at_z(NEAR)))
    x3m = go(remote(fs.at[dest(-3)], c3m, rf_s.at[3], rf_r.at[3], at_z(-NEAR)))
    x1p = go(remote(fs.at[dest(1)], c1p, rf_s.at[4], rf_r.at[4], at_z(NEAR)))
    x1m = go(remote(fs.at[dest(-1)], c1m, rf_s.at[5], rf_r.at[5], at_z(-NEAR)))
    fw1 = forwards(1, IN, ys1)
    x3p.wait_recv()
    x4l.wait_recv()
    v = ff[dest(2)] + c3p[...].astype(F32)
    e2p[:, :H] = (v[:, :H] + c4l[...].astype(F32)).astype(BF)
    e2p[:, H:] = v[:, H:].astype(BF)
    x2p = go(remote(e2p, c2p, rf_s.at[6], rf_r.at[6], at_z(2 * NEAR)))
    x3m.wait_recv()
    x4h.wait_recv()
    v = ff[dest(-2)] + c3m[...].astype(F32)
    e2m[:, :H] = v[:, :H].astype(BF)
    e2m[:, H:] = (v[:, H:] + c4h[...].astype(F32)).astype(BF)
    x2m = go(remote(e2m, c2m, rf_s.at[7], rf_r.at[7], at_z(-2 * NEAR)))
    for cp in fw1:
        cp.wait_recv()
    dwg[...] = lax.dot_general(gg[...], IN[...], TN, preferred_element_type=F32).astype(BF)
    dwu[...] = lax.dot_general(gu[...], IN[...], TN, preferred_element_type=F32).astype(BF)
    total = ff[zh]
    for cp, ref in ((x1p, c1p), (x1m, c1m), (x2p, c2p), (x2m, c2m)):
        cp.wait_recv()
        total = total + ref[...].astype(F32)
    gi[...] = total.astype(BF)

    for cp in pending:
        cp.wait_send()


def store(*refs):
    for src, dst in zip(refs[:4], refs[4:]):
        dst[...] = src[...]


def local(inputs, grad_out, gate, up, gate_weight, up_weight, down_weight):
    anyspec = pl.BlockSpec(memory_space=pl.ANY)
    V = pltpu.VMEM
    dma = pltpu.SemaphoreType.DMA
    four = V((TOK, D), BF)
    scratch = [
        V((FAR, TOK, D), BF), V((FAR, TOK, D), BF),
        V((TOKENS, D), BF), V((TOKENS, D), BF),
        V((F, D), BF), V((F, D), BF), V((F, D), BF),
        V((TOKENS, F), BF), V((TOKENS, F), BF),
        V((TOKENS, F), F32), V((TOKENS, F), F32), V((TOKENS, F), BF),
        V((ROWS, EB, F), BF), V((ROWS, 2 * EB, F), BF), V((ROWS, EB, F), BF),
        V((ROWS, EB, F), BF), V((ROWS, 2 * EB, F), BF), V((ROWS, EB, F), BF),
        V((ROWS, EB, F), BF), V((ROWS, 2 * EB, F), BF), V((ROWS, EB, F), BF),
        V((TOKENS, F), BF), V((TOKENS, F), BF),
        V((YB, D), BF), V((YB, D), BF), V((YB, D), BF),
        V((YB, D), BF), V((YB, D), BF), V((YB, D), BF),
        V((YB, D), F32), V((YB, D), BF),
        V((PB, D), BF), V((PB, D), BF), V((PB, H), BF), V((PB, H), BF),
        V((FAR, TOK, D), BF), V((FAR, TOK, D), F32),
        four, four, four, four, four, four, V((TOK, H), BF), V((TOK, H), BF), four, four,
        dma((7,)),
        dma((2, 4)), dma((2, 4)), dma((2, 2, 2)), dma((2, 2, 2)), dma((2, 4)), dma((2, 4)),
        dma((2, 4, 2)), dma((2, 4, 2)), dma((2, 4, 2)), dma((2, 4, 2)),
        dma((2, ROWS)), dma((2, ROWS)), dma((3, ROWS)), dma((3, ROWS)), dma((3, ROWS)), dma((3, ROWS)),
        dma((6,)), dma((6,)), dma((4,)), dma((4,)), dma((8,)), dma((8,)),
    ]
    shapes = (
        jax.ShapeDtypeStruct((TOK, D), BF),
        jax.ShapeDtypeStruct((F, D), BF),
        jax.ShapeDtypeStruct((F, D), BF),
        jax.ShapeDtypeStruct((F, D), BF),
    )
    vm = pl.BlockSpec(memory_space=pltpu.VMEM)
    args = (inputs, grad_out, gate, up, gate_weight.T, up_weight.T, down_weight)
    made = pl.pallas_call(
        kernel,
        out_shape=shapes,
        in_specs=[anyspec] * 7,
        out_specs=[vm] * 4,
        scratch_shapes=scratch,
        compiler_params=pltpu.CompilerParams(
            collective_id=0, has_side_effects=True, vmem_limit_bytes=40 * 1024 * 1024
        ),
    )(*[pltpu.with_memory_space_constraint(x, pltpu.HBM) for x in args])
    gi, dwg, dwu, dwd = pl.pallas_call(
        store,
        out_shape=shapes,
        in_specs=[vm] * 4,
        out_specs=[vm] * 4,
    )(*[pltpu.with_memory_space_constraint(x, pltpu.VMEM) for x in made])
    return gi, dwg.T, dwu.T, dwd


def solution(mesh):
    return jax.shard_map(
        local,
        mesh=mesh,
        in_specs=(
            P("col", "row"), P("col", "row"), P("row", "col"), P("row", "col"),
            P("row", "col"), P("row", "col"), P("col", "row"),
        ),
        out_specs=(P("col", "row"), P("row", "col"), P("row", "col"), P("col", "row")),
        check_vma=False,
    )
```

time: 110 us -> 94.7 us (0.86)
  Pallas kernels: 102 us -> 93.4 us
  local copies, waits for them, and re-layouts: 5.63 us -> 0 us
    pallas_call x1 -> x2, Pallas kernels: 102 us -> 93.4 us  [the longest x1 92.2 us: local(): pl.pallas_call(kernel, out_shape=shapes, in_specs=[anyspec] * 7, out_spec...]
    unnamed x16 -> x0, local copies, waits for them, and re-layouts: 3.67 us -> none
    pallas_call x2 -> x0, local copies, waits for them, and re-layouts: 1.96 us -> none  [local(): pl.pallas_call(kernel, out_shape=(jax.ShapeDtypeStruct((TOK, D), BF), jax...]
where the time goes in v2:
time: 94.7 us; the launch traced here: 94 us
  Pallas kernels  93.4 us (99%)
    pallas_call x1, Pallas kernels, local(): pl.pallas_call(kernel, out_shape=shapes, in_specs=[anyspec] * 7, out_spec...  92.2 us

profile of v2, /device:TPU:24, one launch (start us, length us, event | category | flops | bytes accessed | tf_op | source)
XLA Modules:
  0.0 94.0 jit_solution(2839669854408001973)
XLA Ops:
  0.6 92.2 %shard_map.102 = (bf16[4,1024]{1,0:T(4,128)(2,1)S(1)}, bf16[240,1024]{1,0:T(8,128)(2,1)S(1)}, bf16[240,1024]{1,0:T(8,128)(2,1)S(1)}, bf16[240,1024]{1,0:T(8,128)(2,1)S(1)}) custom-call(bf16[4,1024]{1,0:T(4,128)(2,1)} %in_hbm.1, bf16[4,1024]{1,0:T(4,128)(2,1)} %out_hbm.1, bf16[64,240]{1,0:T(8,128)(2,1)} %gate_hbm.1, bf16[64,240]{1,0:T(8,128)(2,1)} %up_hbm.1, ...), custom_call_target="tpu_custom_call" | custom-call | tf_op jit(solution)/shard_map/pallas_call | solution.py:393
  92.8 1.2 %shard_map.103 = (bf16[4,1024]{1,0:T(4,128)(2,1)}, bf16[240,1024]{1,0:T(8,128)(2,1)}, bf16[240,1024]{1,0:T(8,128)(2,1)}, bf16[240,1024]{1,0:T(8,128)(2,1)}) custom-call(bf16[4,1024]{1,0:T(4,128)(2,1)S(1)} %get-tuple-element.12.refs_0_, bf16[240,1024]{1,0:T(8,128)(2,1)S(1)} %get-tuple-element.13.refs_1_, bf16[240,1024]{1,0:T(8,128)(2,1)S(1)} %get-tuple-element.14.refs_2_, ...), custom_call_target="tpu_custom_call" | custom-call | tf_op jit(solution)/shard_map/pallas_call | solution.py:403

commit v3 on v2

v3 whole, which is shorter than its diff:
```python
import jax
import jax.numpy as jnp
from jax import lax
from jax.experimental import pallas as pl
from jax.experimental.pallas import tpu as pltpu
from jax.sharding import PartitionSpec as P

MESH = pl.DeviceIdType.MESH
BF = jnp.bfloat16
F32 = jnp.float32

ROWS = 8
NY, NZ = 4, 32
NEAR, FAR = 4, 8
TOK = 4
TOKENS = 512
D = 1024
F = 240
H = D // 2
YB = 128
PB = 32
RB = 64
EB = YB // 8


NT = (((1,), (1,)), ((), ()))
TN = (((0,), (0,)), ((), ()))


def al(x, n):
    return pl.multiple_of(x, n)


def kernel(
    in_hbm, out_hbm, gate_hbm, up_hbm, wg_hbm, wu_hbm, wd_hbm,
    gi, dwg, dwu, dwd,
    o4, i4, OUT, IN, wg, wu, wd, gate, up, fa, fb, hid,
    hp0, hpa, hpb, hr0, hra, hrb, gh0, gha, ghb, gg, gu, s2, sp, sm, r2, rm, rp, tb, sn, n1, n2, n3, n4,
    fs, ff, c1p, c1m, c2p, c2m, c3p, c3m, c4l, c4h, e2p, e2m,
    ld_sem,
    far_s, far_r, fw_s, fw_r, q_s, q_r, near_s, near_r, y_s, y_r, f_s, f_r,
    gu_s, gu_r, hp_s, hp_r, gh_s, gh_r,
    ry_s, ry_r, rn_s, rn_r, rf_s, rf_r,
):
    r = lax.axis_index("row")
    c = lax.axis_index("col")
    y = c // NZ
    z = c % NZ

    def at_z(dz):
        return (r, y * NZ + (z + dz + NZ) % NZ)

    def at_y(dy, dz=0):
        return (r, ((y + dy + NY) % NY) * NZ + (z + dz + NZ) % NZ)

    def at_row(dr):
        return ((r + dr) % ROWS, c)

    def remote(src, dst, ss, rs, dev):
        return pltpu.make_async_remote_copy(
            src_ref=src, dst_ref=dst, send_sem=ss, recv_sem=rs, device_id=dev, device_id_type=MESH
        )

    barrier = pltpu.get_barrier_semaphore()
    partners = [at_z(d) for d in (8, -8, 4, -4, 2, -2, 1, -1)] + [at_y(d) for d in (2, 1, -1)]
    partners += [at_y(dy, dz) for dy in (2, 1, -1) for dz in (2, -2, 1, -1)]
    partners += [at_row(k) for k in range(1, ROWS)]
    for dev in partners:
        pl.semaphore_signal(barrier, inc=1, device_id=dev, device_id_type=MESH)

    loads = [
        pltpu.make_async_copy(out_hbm, o4.at[0, 0, 2], ld_sem.at[0]),
        pltpu.make_async_copy(gate_hbm, gate.at[pl.ds(al(r * RB, RB), RB), :], ld_sem.at[1]),
        pltpu.make_async_copy(up_hbm, up.at[pl.ds(al(r * RB, RB), RB), :], ld_sem.at[2]),
        pltpu.make_async_copy(in_hbm, i4.at[0, 0, 2], ld_sem.at[3]),
        pltpu.make_async_copy(wd_hbm, wd, ld_sem.at[4]),
        pltpu.make_async_copy(wg_hbm, wg, ld_sem.at[5]),
        pltpu.make_async_copy(wu_hbm, wu, ld_sem.at[6]),
    ]
    for cp in loads:
        cp.start()
    loads[0].wait()
    pl.semaphore_wait(barrier, len(partners))

    pending = []

    def go(cp):
        cp.start()
        pending.append(cp)
        return cp

    LO, HI = pl.ds(0, H), pl.ds(H, H)

    DY = (0, -1, 1, 2)
    FIRST, LAST, SHIFTED, ALLF = pl.ds(0, 5), pl.ds(5, 3), pl.ds(4, 3), pl.ds(0, FAR)

    def far_direct(a, buf):
        return [
            go(remote(buf.at[0, 0, 2], buf.at[0, 0, slot], far_s.at[a, j], far_r.at[a, j], at_z(NEAR * d)))
            for j, (d, slot) in enumerate(((2, 0), (-2, 4), (1, 1), (-1, 3)))
        ]

    def far_forward(a, buf, direct):
        out = []
        for j, (d, src, dst, cols) in enumerate(((1, 0, 7, LO), (-1, 4, 5, HI))):
            direct[j].wait_recv()
            out.append(
                go(remote(buf.at[0, 0, src], buf.at[0, 0, dst], fw_s.at[a, j, 0], fw_r.at[a, j, 0], at_z(NEAR * d)))
            )
            out.append(
                go(
                    remote(
                        buf.at[0, 0, src, :, cols], buf.at[0, 0, 6, :, cols],
                        fw_s.at[a, j, 1], fw_r.at[a, j, 1], at_z(2 * NEAR * d),
                    )
                )
            )
        return out

    def near_send(a, buf, part):
        return [
            go(remote(buf.at[0, 0, part], buf.at[0, p, part], near_s.at[a, p], near_r.at[a, p], at_z(dz)))
            for p, dz in ((1, 1), (2, -1), (3, 2))
        ]

    def y_send(a, buf, part, p):
        return [
            go(remote(buf.at[0, p, part], buf.at[b, p, part], y_s.at[a, p, j], y_r.at[a, p, j], at_y(dy)))
            for j, (b, dy) in enumerate(((1, 1), (2, -1)))
        ]

    def y_forward(a, buf, part, ys):
        out = []
        for p in range(NEAR):
            for j, (b, dy, cols) in enumerate(((1, 1, LO), (2, -1, HI))):
                ys[p][j].wait_recv()
                out.append(
                    go(
                        remote(
                            buf.at[b, p, part, :, cols], buf.at[3, p, part, :, cols],
                            f_s.at[a, p, j], f_r.at[a, p, j], at_y(dy),
                        )
                    )
                )
        return out

    def near_to_y(a, buf, part, near):
        ys = [y_send(a, buf, part, 0)]
        for p in (1, 2, 3):
            near[p - 1].wait_recv()
            ys.append(y_send(a, buf, part, p))
        return ys

    def merge(buf, full, b, half):
        for p in range(NEAR):
            block = jnp.concatenate([buf[b, p, 4 * half + j].astype(F32) for j in range(4)], axis=0)
            at = b * YB + p * PB + half * 4 * TOK
            full[at:at + 4 * TOK, :] = block.astype(BF)

    far0 = far_direct(0, o4)

    loads[1].wait()
    loads[2].wait()
    mine = pl.ds(al(r * RB, RB), RB)
    gus = []
    for a, ref in enumerate((gate, up)):
        for k in range(1, ROWS):
            gus.append(go(remote(ref.at[mine, :], ref.at[mine, :], gu_s.at[a, k], gu_r.at[a, k], at_row(k))))

    ffw0 = far_forward(0, o4, far0)
    far0[2].wait_recv()
    far0[3].wait_recv()
    near0 = near_send(0, o4, FIRST)
    ys0 = near_to_y(0, o4, FIRST, near0)
    merge(o4, OUT, 0, 0)
    for cp in ffw0:
        cp.wait_recv()
    rest = [[None] * NEAR for _ in range(NY)]
    for b, dy in ((3, 2), (1, 1), (2, -1), (0, 0)):
        for p, dz, part in ((3, -2, SHIFTED), (1, 1, LAST), (2, -1, LAST), (0, 0, LAST)):
            if b or p:
                rest[b][p] = go(
                    remote(o4.at[0, 0, part], o4.at[b, p, LAST], q_s.at[b, p], q_r.at[b, p], at_y(dy, dz))
                )
    fw0 = y_forward(0, o4, FIRST, ys0)
    merge(o4, OUT, 1, 0)
    merge(o4, OUT, 2, 0)

    for cp in gus:
        cp.wait_recv()
    ri = lax.broadcasted_iota(jnp.int32, (YB, YB), 0)
    ci = lax.broadcasted_iota(jnp.int32, (YB, YB), 1)
    near_i = ri // PB
    step = jnp.where(near_i == 0, 0, jnp.where(near_i == 1, -1, jnp.where(near_i == 2, 1, -2)))
    want = ((z + step + NEAR * ((ri // TOK) % FAR - 2) + 2 * NZ) % NZ) * TOK + ri % TOK
    perm = jnp.where(ci == want, 1.0, 0.0).astype(BF)
    for b in range(NY):
        src = pl.ds(al(((y + DY[b] + NY) % NY) * YB, YB), YB)
        rows = pl.ds(b * YB, YB)
        g = jnp.dot(perm, gate[src, :], preferred_element_type=F32)
        u = jnp.dot(perm, up[src, :], preferred_element_type=F32)
        s = 1.0 / (1.0 + jnp.exp(-g))
        act = g * s
        fa[rows, :] = u * s * (1.0 + g * (1.0 - s))
        fb[rows, :] = act
        hid[rows, :] = (act * u).astype(BF)

    loads[4].wait()

    def y_rows(b):
        return pl.ds(b * YB, YB)

    def arrived(b):
        for cp in rest[b]:
            if cp is not None:
                cp.wait_recv()
        merge(o4, OUT, b, 1)

    def hidden_block(b, dst, i):
        part = lax.dot_general(OUT[y_rows(b), :], wd[...], NT, preferred_element_type=F32)
        dst[:, i * EB:(i + 1) * EB, :] = part.astype(BF).reshape(ROWS, EB, F)

    def row_out(src, dst, b):
        cps = []
        for k in range(1, ROWS):
            cps.append(go(remote(src.at[(r + k) % ROWS], dst.at[k], hp_s.at[b, k], hp_r.at[b, k], at_row(k))))
        return cps

    def row_back(cps, own, got, dst, b):
        acc = own[r].astype(F32)
        for k in range(1, ROWS):
            cps[k - 1].wait_recv()
            acc = acc + got[k].astype(F32)
        dst[r] = acc.astype(BF)
        return [go(remote(dst.at[r], dst.at[r], gh_s.at[b, k], gh_r.at[b, k], at_row(k))) for k in range(1, ROWS)]

    def gated(b, src, i):
        rows = y_rows(b)
        v = src[:, i * EB:(i + 1) * EB, :].reshape(YB, F).astype(F32)
        gg[rows, :] = (v * fa[rows, :]).astype(BF)
        gu[rows, :] = (v * fb[rows, :]).astype(BF)

    def partial(b):
        rows = y_rows(b)
        return jnp.dot(gg[rows, :], wg[...], preferred_element_type=F32) + jnp.dot(
            gu[rows, :], wu[...], preferred_element_type=F32
        )

    arrived(0)
    hidden_block(0, hp0, 0)
    x0 = row_out(hp0, hr0, 0)
    arrived(1)
    hidden_block(1, hpa, 0)
    arrived(2)
    hidden_block(2, hpa, 1)
    xa = row_out(hpa, hra, 1)
    loads[3].wait()
    far1 = far_direct(1, i4)
    for cp in fw0:
        cp.wait_recv()
    merge(o4, OUT, 3, 0)
    arrived(3)
    hidden_block(3, hpb, 0)
    xb = row_out(hpb, hrb, 2)
    g0 = row_back(x0, hp0, hr0, gh0, 0)
    ga = row_back(xa, hpa, hra, gha, 1)
    gb = row_back(xb, hpb, hrb, ghb, 2)
    ffw1 = far_forward(1, i4, far1)

    loads[5].wait()
    loads[6].wait()
    for cp in ga:
        cp.wait_recv()
    gated(2, gha, 1)
    sp[...] = partial(2).astype(BF)
    go_p = go(remote(sp, rm, ry_s.at[0], ry_r.at[0], at_y(1)))
    gated(1, gha, 0)
    sm[...] = partial(1).astype(BF)
    go_m = go(remote(sm, rp, ry_s.at[1], ry_r.at[1], at_y(-1)))
    for cp in g0:
        cp.wait_recv()
    gated(0, gh0, 0)
    tb[...] = partial(0)
    for cp in gb:
        cp.wait_recv()
    gated(3, ghb, 0)

    def local_piece(p):
        return pl.ds(p * PB, PB)

    RQ = (3, 2, 1, 0)
    s2[...] = partial(3).astype(BF)
    far_y = [
        go(remote(s2.at[local_piece(q), :], r2.at[local_piece(q), :], ry_s.at[2 + i], ry_r.at[2 + i], at_y(2)))
        for i, q in enumerate(RQ)
    ]
    for cp in far1[2:] + ffw1:
        cp.wait_recv()
    near1 = near_send(1, i4, ALLF)
    dwd[...] = lax.dot_general(hid[...], OUT[...], TN, preferred_element_type=F32).astype(BF)

    go_p.wait_recv()
    go_m.wait_recv()
    tb[...] = tb[...] + rm[...].astype(F32) + rp[...].astype(F32)
    nx = []
    for i, q in enumerate(RQ):
        rows = local_piece(q)
        far_y[i].wait_recv()
        v = tb[rows, :] + r2[rows, :].astype(F32)
        if q == 0:
            tb[rows, :] = v
            continue
        if q == 3:
            sn[rows, :H] = jnp.concatenate([v[TOK:, :H], v[:TOK, :H]], axis=0).astype(BF)
            sn[rows, H:] = v[:, H:].astype(BF)
            nx.append(go(remote(sn.at[rows, LO], n3, rn_s.at[2], rn_r.at[2], at_z(2))))
            nx.append(go(remote(sn.at[rows, HI], n4, rn_s.at[3], rn_r.at[3], at_z(-2))))
            continue
        sn[rows, :] = v.astype(BF)
        if q == 2:
            nx.append(go(remote(sn.at[rows, :], n1, rn_s.at[0], rn_r.at[0], at_z(1))))
        else:
            nx.append(go(remote(sn.at[rows, :], n2, rn_s.at[1], rn_r.at[1], at_z(-1))))

    ys1 = near_to_y(1, i4, ALLF, near1)
    for cp in nx:
        cp.wait_recv()
    own = tb[local_piece(0), :] + n1[...].astype(F32) + n2[...].astype(F32)
    lo = own[:, :H] + n3[...].astype(F32)
    hi = own[:, H:] + n4[...].astype(F32)
    for k in range(FAR):
        ff[k, :, :H] = lo[k * TOK:(k + 1) * TOK, :]
        ff[k, :, H:] = hi[k * TOK:(k + 1) * TOK, :]
    for k in range(FAR):
        fs[k] = ff[k].astype(BF)

    def dest(d):
        return (d + 2) % FAR

    x4l = go(remote(fs.at[dest(4), :, LO], c4l, rf_s.at[0], rf_r.at[0], at_z(2 * NEAR)))
    x4h = go(remote(fs.at[dest(4), :, HI], c4h, rf_s.at[1], rf_r.at[1], at_z(-2 * NEAR)))
    x3p = go(remote(fs.at[dest(3)], c3p, rf_s.at[2], rf_r.at[2], at_z(NEAR)))
    x3m = go(remote(fs.at[dest(-3)], c3m, rf_s.at[3], rf_r.at[3], at_z(-NEAR)))
    x1p = go(remote(fs.at[dest(1)], c1p, rf_s.at[4], rf_r.at[4], at_z(NEAR)))
    x1m = go(remote(fs.at[dest(-1)], c1m, rf_s.at[5], rf_r.at[5], at_z(-NEAR)))
    fw1 = y_forward(1, i4, ALLF, ys1)
    x3p.wait_recv()
    x4l.wait_recv()
    v = ff[dest(2)] + c3p[...].astype(F32)
    e2p[:, :H] = (v[:, :H] + c4l[...].astype(F32)).astype(BF)
    e2p[:, H:] = v[:, H:].astype(BF)
    x2p = go(remote(e2p, c2p, rf_s.at[6], rf_r.at[6], at_z(2 * NEAR)))
    x3m.wait_recv()
    x4h.wait_recv()
    v = ff[dest(-2)] + c3m[...].astype(F32)
    e2m[:, :H] = v[:, :H].astype(BF)
    e2m[:, H:] = (v[:, H:] + c4h[...].astype(F32)).astype(BF)
    x2m = go(remote(e2m, c2m, rf_s.at[7], rf_r.at[7], at_z(-2 * NEAR)))
    for cp in fw1:
        cp.wait_recv()
    for b in range(NY):
        merge(i4, IN, b, 0)
        merge(i4, IN, b, 1)
    dwg[...] = lax.dot_general(gg[...], IN[...], TN, preferred_element_type=F32).astype(BF)
    dwu[...] = lax.dot_general(gu[...], IN[...], TN, preferred_element_type=F32).astype(BF)
    total = ff[2]
    for cp, ref in ((x1p, c1p), (x1m, c1m), (x2p, c2p), (x2m, c2m)):
        cp.wait_recv()
        total = total + ref[...].astype(F32)
    gi[...] = total.astype(BF)

    for cp in pending:
        cp.wait_send()


def store(*refs):
    for src, dst in zip(refs[:4], refs[4:]):
        dst[...] = src[...]


def local(inputs, grad_out, gate, up, gate_weight, up_weight, down_weight):
    anyspec = pl.BlockSpec(memory_space=pl.ANY)
    V = pltpu.VMEM
    dma = pltpu.SemaphoreType.DMA
    four = V((TOK, D), BF)
    scratch = [
        V((NY, NEAR, FAR, TOK, D), BF), V((NY, NEAR, FAR, TOK, D), BF),
        V((TOKENS, D), BF), V((TOKENS, D), BF),
        V((F, D), BF), V((F, D), BF), V((F, D), BF),
        V((TOKENS, F), BF), V((TOKENS, F), BF),
        V((TOKENS, F), F32), V((TOKENS, F), F32), V((TOKENS, F), BF),
        V((ROWS, EB, F), BF), V((ROWS, 2 * EB, F), BF), V((ROWS, EB, F), BF),
        V((ROWS, EB, F), BF), V((ROWS, 2 * EB, F), BF), V((ROWS, EB, F), BF),
        V((ROWS, EB, F), BF), V((ROWS, 2 * EB, F), BF), V((ROWS, EB, F), BF),
        V((TOKENS, F), BF), V((TOKENS, F), BF),
        V((YB, D), BF), V((YB, D), BF), V((YB, D), BF),
        V((YB, D), BF), V((YB, D), BF), V((YB, D), BF),
        V((YB, D), F32), V((YB, D), BF),
        V((PB, D), BF), V((PB, D), BF), V((PB, H), BF), V((PB, H), BF),
        V((FAR, TOK, D), BF), V((FAR, TOK, D), F32),
        four, four, four, four, four, four, V((TOK, H), BF), V((TOK, H), BF), four, four,
        dma((7,)),
        dma((2, 4)), dma((2, 4)), dma((2, 2, 2)), dma((2, 2, 2)), dma((4, 4)), dma((4, 4)), dma((2, 4)), dma((2, 4)),
        dma((2, 4, 2)), dma((2, 4, 2)), dma((2, 4, 2)), dma((2, 4, 2)),
        dma((2, ROWS)), dma((2, ROWS)), dma((3, ROWS)), dma((3, ROWS)), dma((3, ROWS)), dma((3, ROWS)),
        dma((6,)), dma((6,)), dma((4,)), dma((4,)), dma((8,)), dma((8,)),
    ]
    shapes = (
        jax.ShapeDtypeStruct((TOK, D), BF),
        jax.ShapeDtypeStruct((F, D), BF),
        jax.ShapeDtypeStruct((F, D), BF),
        jax.ShapeDtypeStruct((F, D), BF),
    )
    vm = pl.BlockSpec(memory_space=pltpu.VMEM)
    args = (inputs, grad_out, gate, up, gate_weight.T, up_weight.T, down_weight)
    made = pl.pallas_call(
        kernel,
        out_shape=shapes,
        in_specs=[anyspec] * 7,
        out_specs=[vm] * 4,
        scratch_shapes=scratch,
        compiler_params=pltpu.CompilerParams(
            collective_id=0, has_side_effects=True, vmem_limit_bytes=40 * 1024 * 1024
        ),
    )(*[pltpu.with_memory_space_constraint(x, pltpu.HBM) for x in args])
    gi, dwg, dwu, dwd = pl.pallas_call(
        store,
        out_shape=shapes,
        in_specs=[vm] * 4,
        out_specs=[vm] * 4,
    )(*[pltpu.with_memory_space_constraint(x, pltpu.VMEM) for x in made])
    return gi, dwg.T, dwu.T, dwd


def solution(mesh):
    return jax.shard_map(
        local,
        mesh=mesh,
        in_specs=(
            P("col", "row"), P("col", "row"), P("row", "col"), P("row", "col"),
            P("row", "col"), P("row", "col"), P("col", "row"),
        ),
        out_specs=(P("col", "row"), P("row", "col"), P("row", "col"), P("col", "row")),
        check_vma=False,
    )
```

time: 94.7 us -> 91.6 us (0.967)
  Pallas kernels: 93.4 us -> 90.8 us
    pallas_call x1, Pallas kernels: 92.2 us -> 89.6 us  [local(): pl.pallas_call(kernel, out_shape=shapes, in_specs=[anyspec] * 7, out_spec...]
where the time goes in v3:
time: 91.6 us; the launch traced here: 91.5 us
  Pallas kernels  90.8 us (99%)
    pallas_call x1, Pallas kernels, local(): pl.pallas_call(kernel, out_shape=shapes, in_specs=[anyspec] * 7, out_spec...  89.6 us

profile of v3, /device:TPU:24, one launch (start us, length us, event | category | flops | bytes accessed | tf_op | source)
XLA Modules:
  0.0 91.5 jit_solution(833205807751578089)
XLA Ops:
  0.6 89.6 %shard_map.102 = (bf16[4,1024]{1,0:T(4,128)(2,1)S(1)}, bf16[240,1024]{1,0:T(8,128)(2,1)S(1)}, bf16[240,1024]{1,0:T(8,128)(2,1)S(1)}, bf16[240,1024]{1,0:T(8,128)(2,1)S(1)}) custom-call(bf16[4,1024]{1,0:T(4,128)(2,1)} %in_hbm.1, bf16[4,1024]{1,0:T(4,128)(2,1)} %out_hbm.1, bf16[64,240]{1,0:T(8,128)(2,1)} %gate_hbm.1, bf16[64,240]{1,0:T(8,128)(2,1)} %up_hbm.1, ...), custom_call_target="tpu_custom_call" | custom-call | tf_op jit(solution)/shard_map/pallas_call | solution.py:416
  90.3 1.2 %shard_map.103 = (bf16[4,1024]{1,0:T(4,128)(2,1)}, bf16[240,1024]{1,0:T(8,128)(2,1)}, bf16[240,1024]{1,0:T(8,128)(2,1)}, bf16[240,1024]{1,0:T(8,128)(2,1)}) custom-call(bf16[4,1024]{1,0:T(4,128)(2,1)S(1)} %get-tuple-element.12.refs_0_, bf16[240,1024]{1,0:T(8,128)(2,1)S(1)} %get-tuple-element.13.refs_1_, bf16[240,1024]{1,0:T(8,128)(2,1)S(1)} %get-tuple-element.14.refs_2_, ...), custom_call_target="tpu_custom_call" | custom-call | tf_op jit(solution)/shard_map/pallas_call | solution.py:426

commit v4 on v3

--- a/solution.py
+++ b/solution.py
@@ -35,7 +35,7 @@
     in_hbm, out_hbm, gate_hbm, up_hbm, wg_hbm, wu_hbm, wd_hbm,
     gi, dwg, dwu, dwd,
     o4, i4, OUT, IN, wg, wu, wd, gate, up, fa, fb, hid,
-    hp0, hpa, hpb, hr0, hra, hrb, gh0, gha, ghb, gg, gu, s2, sp, sm, r2, rm, rp, tb, sn, n1, n2, n3, n4,
+    hp0, hpa, hpb, hr0, hra, hrb, gh0, gha, ghb, gg, gu, s2, sp, sm, r2, rm, rp, tp, tm, tb, sn, n1, n2, n3, n4,
     fs, ff, c1p, c1m, c2p, c2m, c3p, c3m, c4l, c4h, e2p, e2m,
     ld_sem,
     far_s, far_r, fw_s, fw_r, q_s, q_r, near_s, near_r, y_s, y_r, f_s, f_r,
@@ -272,11 +272,13 @@
     for cp in ga:
         cp.wait_recv()
     gated(2, gha, 1)
-    sp[...] = partial(2).astype(BF)
-    go_p = go(remote(sp, rm, ry_s.at[0], ry_r.at[0], at_y(1)))
+    tp[...] = partial(2)
+    sp[:, H:] = tp[:, H:].astype(BF)
+    go_p = go(remote(sp.at[:, HI], rm.at[:, HI], ry_s.at[0], ry_r.at[0], at_y(1)))
     gated(1, gha, 0)
-    sm[...] = partial(1).astype(BF)
-    go_m = go(remote(sm, rp, ry_s.at[1], ry_r.at[1], at_y(-1)))
+    tm[...] = partial(1)
+    sm[:, :H] = tm[:, :H].astype(BF)
+    go_m = go(remote(sm.at[:, LO], rp.at[:, LO], ry_s.at[1], ry_r.at[1], at_y(-1)))
     for cp in g0:
         cp.wait_recv()
     gated(0, gh0, 0)
@@ -290,10 +292,25 @@
 
     RQ = (3, 2, 1, 0)
     s2[...] = partial(3).astype(BF)
-    far_y = [
-        go(remote(s2.at[local_piece(q), :], r2.at[local_piece(q), :], ry_s.at[2 + i], ry_r.at[2 + i], at_y(2)))
-        for i, q in enumerate(RQ)
-    ]
+    half_y = []
+    for i, q in enumerate(RQ):
+        rows = local_piece(q)
+        half_y.append(
+            [
+                go(remote(s2.at[rows, cols], r2.at[rows, cols], ry_s.at[2 + 2 * i + j], ry_r.at[2 + 2 * i + j], at_y(dy)))
+                for j, (cols, dy) in enumerate(((LO, 1), (HI, -1)))
+            ]
+        )
+    far_y = []
+    for i, q in enumerate(RQ):
+        rows = local_piece(q)
+        half_y[i][0].wait_recv()
+        sp[rows, :H] = (tp[rows, :H] + r2[rows, :H].astype(F32)).astype(BF)
+        one = go(remote(sp.at[rows, LO], rm.at[rows, LO], ry_s.at[10 + 2 * i], ry_r.at[10 + 2 * i], at_y(1)))
+        half_y[i][1].wait_recv()
+        sm[rows, H:] = (tm[rows, H:] + r2[rows, H:].astype(F32)).astype(BF)
+        two = go(remote(sm.at[rows, HI], rp.at[rows, HI], ry_s.at[11 + 2 * i], ry_r.at[11 + 2 * i], at_y(-1)))
+        far_y.append((one, two))
     for cp in far1[2:] + ffw1:
         cp.wait_recv()
     near1 = near_send(1, i4, ALLF)
@@ -301,12 +318,12 @@
 
     go_p.wait_recv()
     go_m.wait_recv()
-    tb[...] = tb[...] + rm[...].astype(F32) + rp[...].astype(F32)
     nx = []
     for i, q in enumerate(RQ):
         rows = local_piece(q)
-        far_y[i].wait_recv()
-        v = tb[rows, :] + r2[rows, :].astype(F32)
+        far_y[i][0].wait_recv()
+        far_y[i][1].wait_recv()
+        v = tb[rows, :] + rm[rows, :].astype(F32) + rp[rows, :].astype(F32)
         if q == 0:
             tb[rows, :] = v
             continue
@@ -395,7 +412,7 @@
         V((TOKENS, F), BF), V((TOKENS, F), BF),
         V((YB, D), BF), V((YB, D), BF), V((YB, D), BF),
         V((YB, D), BF), V((YB, D), BF), V((YB, D), BF),
-        V((YB, D), F32), V((YB, D), BF),
+        V((YB, D), F32), V((YB, D), F32), V((YB, D), F32), V((YB, D), BF),
         V((PB, D), BF), V((PB, D), BF), V((PB, H), BF), V((PB, H), BF),
         V((FAR, TOK, D), BF), V((FAR, TOK, D), F32),
         four, four, four, four, four, four, V((TOK, H), BF), V((TOK, H), BF), four, four,
@@ -403,7 +420,7 @@
         dma((2, 4)), dma((2, 4)), dma((2, 2, 2)), dma((2, 2, 2)), dma((4, 4)), dma((4, 4)), dma((2, 4)), dma((2, 4)),
         dma((2, 4, 2)), dma((2, 4, 2)), dma((2, 4, 2)), dma((2, 4, 2)),
         dma((2, ROWS)), dma((2, ROWS)), dma((3, ROWS)), dma((3, ROWS)), dma((3, ROWS)), dma((3, ROWS)),
-        dma((6,)), dma((6,)), dma((4,)), dma((4,)), dma((8,)), dma((8,)),
+        dma((18,)), dma((18,)), dma((4,)), dma((4,)), dma((8,)), dma((8,)),
     ]
     shapes = (
         jax.ShapeDtypeStruct((TOK, D), BF),

time: 91.6 us -> 91.4 us (level)
  no operation moved by 1% of the time
where the time goes in v4:
time: 91.4 us; the launch traced here: 91.3 us
  Pallas kernels  90.6 us (99%)
    pallas_call x1, Pallas kernels, local(): pl.pallas_call(kernel, out_shape=shapes, in_specs=[anyspec] * 7, out_spec...  89.4 us

profile of v4, /device:TPU:24, one launch (start us, length us, event | category | flops | bytes accessed | tf_op | source)
XLA Modules:
  0.0 91.3 jit_solution(14463940390045463115)
XLA Ops:
  0.6 89.4 %shard_map.102 = (bf16[4,1024]{1,0:T(4,128)(2,1)S(1)}, bf16[240,1024]{1,0:T(8,128)(2,1)S(1)}, bf16[240,1024]{1,0:T(8,128)(2,1)S(1)}, bf16[240,1024]{1,0:T(8,128)(2,1)S(1)}) custom-call(bf16[4,1024]{1,0:T(4,128)(2,1)} %in_hbm.1, bf16[4,1024]{1,0:T(4,128)(2,1)} %out_hbm.1, bf16[64,240]{1,0:T(8,128)(2,1)} %gate_hbm.1, bf16[64,240]{1,0:T(8,128)(2,1)} %up_hbm.1, ...), custom_call_target="tpu_custom_call" | custom-call | tf_op jit(solution)/shard_map/pallas_call | solution.py:433
  90.0 1.2 %shard_map.103 = (bf16[4,1024]{1,0:T(4,128)(2,1)}, bf16[240,1024]{1,0:T(8,128)(2,1)}, bf16[240,1024]{1,0:T(8,128)(2,1)}, bf16[240,1024]{1,0:T(8,128)(2,1)}) custom-call(bf16[4,1024]{1,0:T(4,128)(2,1)S(1)} %get-tuple-element.12.refs_0_, bf16[240,1024]{1,0:T(8,128)(2,1)S(1)} %get-tuple-element.13.refs_1_, bf16[240,1024]{1,0:T(8,128)(2,1)S(1)} %get-tuple-element.14.refs_2_, ...), custom_call_target="tpu_custom_call" | custom-call | tf_op jit(solution)/shard_map/pallas_call | solution.py:443
